TPU v7x, 32 devices: a whole 2x2x4 slice. The times are simulated.
32 devices in a mesh: space: 4 (over x, core), freq: 8 (over z, y).
Axes of the slice: x: 2, y: 2, z: 4, core: 2. Of those that a mesh axis runs over, the one named last changes fastest.
Arguments:
- spectrum: float32 [32, 36, 128, 256], P('freq', None, 'space'), may hold values from 0.05 to 2
- land_sea: int32 [128, 256], P('space'), may hold values 0 or 1
- courant: float32 [32], P('freq'), may hold values from 0.2 to 0.65
- refract: float32 [32], P('freq'), may hold values from 0.2 to 0.9
- depth_dx: float32 [128, 256], P('space'), may hold values from -0.5 to 0.5
- depth_dy: float32 [128, 256], P('space'), may hold values from -0.5 to 0.5
- w_in: bfloat16 [1152, 2048], P(None, 'freq'), may hold values from -0.1875 to 0.1875
- w_out: bfloat16 [2048, 1152], P('freq'), may hold values from -0.125 to 0.125
Outputs:
- spectrum_out: float32 [32, 36, 128, 256], P('freq', None, 'space')
All inputs are finite; a program needn't handle non-finite values. No bound on the sum of `land_sea` on one device may be relied on, other than what follows from the above.
Results may differ from a plain program's by a relative error of at most 0.003.
Values may be sent and summed in bfloat16 or wider, within the bound.
No kernel may reach another device: no remote copies, remote signals or barrier semaphores. Data moves between devices by JAX's collectives and lax.ppermute only.
A program may use at most 128 MiB of HBM per device.

v0:
```python
import math

import jax
import jax.numpy as jnp
from jax import lax
from jax.sharding import PartitionSpec as P

DIRS = 36
STEPS = 2


step_scale = 0.5
epsilon = 1e-06


def padded_2(block, sides, width):
    for axis, dim in sides:
        count = lax.axis_size(axis)
        forward = [(i, i + 1) for i in range(count - 1)]
        backward = [(target, source) for source, target in forward]
        low = lax.ppermute(
            lax.slice_in_dim(block, block.shape[dim] - width, None, axis=dim), axis, forward
        )
        high = lax.ppermute(lax.slice_in_dim(block, 0, width, axis=dim), axis, backward)
        block = jnp.concatenate([low, block, high], axis=dim)
    return block


def direction_tables():
    angles = (jnp.arange(DIRS, dtype=jnp.float32) + 0.5) * (2.0 * math.pi / DIRS)
    return (jnp.cos(angles), jnp.sin(angles))


def transport(padded, courant, refract, depth_dx, depth_dy, seamask):
    cosine, sine_dir = direction_tables()
    speed_x = courant[:, None] * cosine[None, :]
    speed_y = courant[:, None] * sine_dir[None, :]
    pos_x = jnp.maximum(speed_x, 0.0)[:, :, None, None]
    neg_x = jnp.maximum(-speed_x, 0.0)[:, :, None, None]
    pos_y = jnp.maximum(speed_y, 0.0)[:, :, None, None]
    neg_y = jnp.maximum(-speed_y, 0.0)[:, :, None, None]
    center = padded[:, :, 1:-1, 1:-1]
    keeping = 1.0 - jnp.abs(speed_x)[:, :, None, None] - jnp.abs(speed_y)[:, :, None, None]
    shifted = center * keeping + pos_x * padded[:, :, :-2, 1:-1] + neg_x * padded[:, :, 2:, 1:-1]
    shifted = shifted + pos_y * padded[:, :, 1:-1, :-2] + neg_y * padded[:, :, 1:-1, 2:]
    turn_rate = refract[:, None, None, None] * (
        sine_dir[None, :, None, None] * depth_dx[None, None]
        - cosine[None, :, None, None] * depth_dy[None, None]
    )
    turn_pos = jnp.maximum(turn_rate, 0.0)
    turn_neg = jnp.maximum(-turn_rate, 0.0)
    turned = shifted * (1.0 - jnp.abs(turn_rate)) + jnp.roll(turn_pos * shifted, 1, axis=1)
    turned = turned + jnp.roll(turn_neg * shifted, -1, axis=1)
    return turned * seamask[None, None]


def body(spectrum, land_sea, courant, refract, depth_dx, depth_dy, w_in, w_out):
    contract = (((0,), (0,)), ((), ()))
    seamask = land_sea.astype(jnp.float32)
    groups = lax.axis_size("freq")
    local_freqs, directions, rows, columns = spectrum.shape
    point_rows = rows // groups
    channels = local_freqs * groups * directions
    in_whole, out_whole = (
        lax.all_gather(w_in, "freq", axis=1, tiled=True),
        lax.all_gather(w_out, "freq", axis=0, tiled=True),
    )
    field = spectrum
    for repeat in range(STEPS):
        padded = padded_2(field, (("space", 2),), 1)
        padded = jnp.pad(padded, ((0, 0), (0, 0), (0, 0), (1, 1)))
        field = transport(padded, courant, refract, depth_dx, depth_dy, seamask)
        partial_sum = jnp.sum(field, axis=(0, 1))
        point_total = lax.psum(partial_sum, "freq")
        energy_mean = point_total / channels + epsilon
        scaled = (field / energy_mean[None, None]).astype(jnp.bfloat16)
        arrived = lax.all_to_all(scaled, "freq", split_axis=2, concat_axis=0, tiled=True)
        preact = lax.dot_general(
            in_whole,
            arrived.reshape(channels, point_rows * columns),
            contract,
            preferred_element_type=jnp.float32,
        )
        hidden = jax.nn.gelu(preact).astype(jnp.bfloat16)
        source = lax.dot_general(out_whole, hidden, contract, preferred_element_type=jnp.float32)
        source = source.astype(jnp.bfloat16)
        shaped = source.reshape(local_freqs * groups, directions, point_rows, columns)
        returned = lax.all_to_all(shaped, "freq", split_axis=0, concat_axis=2, tiled=True)
        field = field * jnp.exp(step_scale * jnp.tanh(returned.astype(jnp.float32)))
    return field


def solution(mesh):
    placed = (
        P("freq", None, "space", None),
        P("space", None),
        P("freq"),
        P("freq"),
        P("space", None),
        P("space", None),
        P(None, "freq"),
        P("freq", None),
    )
    return jax.shard_map(
        body, mesh=mesh, in_specs=placed, out_specs=P("freq", None, "space", None), check_vma=False
    )
```

profile of v0, /device:TPU:0, one launch (start us, length us, event | category | flops | bytes accessed | tf_op | source)
XLA Modules:
  0.0 529.1 jit_solution(14539101689349413563)
XLA Ops:
  10.5 3.2 collective-permute-start
  13.8 5.1 copy.17
  19.3 5.4 %select_maximum_fusion.2 = f32[4,36,34,258]{3,1,0,2:T(8,128)} fusion(f32[4,36,1,256]{3,1,0,2:T(8,128)S(1)} %bitcast.70, f32[4,36,32,256]{3,1,0,2:T(8,128)S(1)} %copy.17, f32[4,36,1,256]{3,1,0,2:T(8,128)S(1)} %bitcast.72), kind=kLoop, calls=%fused_computation.25 | loop fusion | flops 10105344 | bytes 10066176 | tf_op jit(solution)/shard_map/concatenate | solution.py:25
  24.7 9.0 %fusion.30 = (f32[4,36,32,256]{3,1,0,2:T(8,128)}, f32[4,36,32,256]{3,1,0,2:T(8,128)}) fusion(f32[36,32,256]{2,0,1:T(8,128)S(1)} %multiply_subtract_fusion, f32[4]{0:T(128)S(1)} %copy-done.3, f32[4,36,34,258]{3,1,0,2:T(8,128)} %select_maximum_fusion.2, f32[4,36]{1,0:T(4,128)S(1)} %get-tuple-element.20, f32[4,36]{1,0:T(4,128)S(1)} %get-tuple-element.21, ...), kind=kLoop, calls=%fused_computation.41 | loop fusion | flops 17694720 | bytes 25070416 | tf_op jit(solution)/shard_map/mul | solution.py:53
  35.1 3.4 slice.100
  39.8 4.6 fusion.62
  44.4 40.7 %psum.14 = f32[32,256]{1,0:T(8,128)S(1)} all-reduce(f32[32,256]{1,0:T(8,128)S(1)} %get-tuple-element.9), channel_id=1, replica_groups=mesh['space'=4,'freq'=8] {'freq'}, use_global_device_ids=true, to_apply=%region_1.2 | all-reduce | flops 8192 | bytes 65536 | tf_op jit(solution)/shard_map/psum | solution.py:74
  88.3 98.2 %all_to_all.48 = bf16[4,36,32,256]{3,1,0,2:T(8,128)(2,1)S(1)} all-to-all(bf16[4,36,32,256]{3,1,0,2:T(8,128)(2,1)S(1)} %divide_convert_fusion.1), channel_id=1, replica_groups=mesh['space'=4,'freq'=8] {'freq'}, dimensions={2} | all-to-all | bytes 4718592 | tf_op jit(solution)/shard_map/all_to_all | solution.py:77
  190.2 17.1 %all-gather.5.cloned.1.call-done = bf16[2048,1152]{1,0:T(8,128)(2,1)} async-done(((bf16[256,1152]{1,0:T(8,128)(2,1)}), bf16[2048,1152]{1,0:T(8,128)(2,1)}) %all-gather.5.cloned.1.call-update) | async-done | bytes 4718608 | tf_op jit(solution)/shard_map/all_gather | solution.py:66
  207.3 18.8 %fusion.43 = bf16[1152,1024]{0,1:T(8,128)(2,1)} fusion(bf16[2048,1152]{1,0:T(8,128)(2,1)} %all-gather.5.cloned.1.call-done, bf16[1152,1024]{1,0:T(8,128)(2,1)} %bitcast.68, bf16[1152,2048]{1,0:T(8,128)(2,1)} %all-gather.3.cloned.1.call-done), kind=kOutput, calls=%fused_computation.70 | convolution fusion | flops 9683730432 | bytes 14155776 | tf_op jit(solution)/shard_map/dot_general | solution.py:85
  226.1 4.3 copy.28
  230.3 5.6 %reshape.233 = bf16[32,36,4,256]{3,2,1,0:T(4,128)(2,1)} reshape(bf16[1152,1024]{1,0:T(8,128)(2,1)} %copy.28) | data formatting | bytes 4718592 | tf_op jit(solution)/shard_map/reshape | solution.py:87
  235.9 57.7 %all_to_all.49 = bf16[32,36,4,256]{3,2,1,0:T(4,128)(2,1)S(1)} all-to-all(bf16[32,36,4,256]{3,2,1,0:T(4,128)(2,1)} %reshape.233), channel_id=1, replica_groups=mesh['space'=4,'freq'=8] {'freq'}, dimensions={0} | all-to-all | bytes 4718592 | tf_op jit(solution)/shard_map/all_to_all | solution.py:88
  302.4 3.4 collective-permute-done.3
  305.8 5.4 %select_maximum_fusion = f32[4,36,34,258]{3,1,0,2:T(8,128)} fusion(f32[4,36,1,256]{3,1,0,2:T(8,128)S(1)} %bitcast.76, f32[4,36,32,256]{3,1,0,2:T(8,128)S(1)} %bitcast_multiply_fusion.1, f32[4,36,1,256]{3,1,0,2:T(8,128)S(1)} %bitcast.74), kind=kLoop, calls=%fused_computation.23 | loop fusion | flops 10105344 | bytes 10066176 | tf_op jit(solution)/shard_map/concatenate | solution.py:25
  311.1 9.0 %fusion.29 = (f32[4,36,32,256]{3,1,0,2:T(8,128)}, f32[4,36,32,256]{3,1,0,2:T(8,128)}) fusion(f32[36,32,256]{2,0,1:T(8,128)S(1)} %multiply_subtract_fusion, f32[4]{0:T(128)S(1)} %copy-done.3, f32[4,36,34,258]{3,1,0,2:T(8,128)} %select_maximum_fusion, f32[4,36]{1,0:T(4,128)S(1)} %get-tuple-element.20, f32[4,36]{1,0:T(4,128)S(1)} %get-tuple-element.21, ...), kind=kLoop, calls=%fused_computation.40 | loop fusion | flops 17694720 | bytes 25070416 | tf_op jit(solution)/shard_map/mul | solution.py:53
  321.6 3.4 slice.108
  326.2 4.6 fusion.59
  330.9 35.2 %psum.15 = f32[32,256]{1,0:T(8,128)S(1)} all-reduce(f32[32,256]{1,0:T(8,128)S(1)} %get-tuple-element.5), channel_id=1, replica_groups=mesh['space'=4,'freq'=8] {'freq'}, use_global_device_ids=true, to_apply=%region_3.4 | all-reduce | flops 8192 | bytes 65536 | tf_op jit(solution)/shard_map/psum | solution.py:74
  366.1 3.2 divide_convert_fusion
  369.2 59.0 %all_to_all.50 = bf16[4,36,32,256]{3,1,0,2:T(8,128)(2,1)S(1)} all-to-all(bf16[4,36,32,256]{3,1,0,2:T(8,128)(2,1)S(1)} %divide_convert_fusion), channel_id=1, replica_groups=mesh['space'=4,'freq'=8] {'freq'}, dimensions={2} | all-to-all | bytes 4718592 | tf_op jit(solution)/shard_map/all_to_all | solution.py:77
  430.6 18.1 %fusion.44 = bf16[1152,1024]{0,1:T(8,128)(2,1)} fusion(bf16[2048,1152]{1,0:T(8,128)(2,1)} %all-gather.5.cloned.1.call-done, bf16[1152,1024]{1,0:T(8,128)(2,1)S(1)} %bitcast.69, bf16[1152,2048]{1,0:T(8,128)(2,1)} %all-gather.3.cloned.1.call-done), kind=kOutput, calls=%fused_computation.71 | convolution fusion | flops 9683730432 | bytes 14155776 | tf_op jit(solution)/shard_map/dot_general | solution.py:85
  454.5 56.5 %all_to_all.51 = bf16[32,36,4,256]{3,2,1,0:T(4,128)(2,1)S(1)} all-to-all(bf16[32,36,4,256]{3,2,1,0:T(4,128)(2,1)} %reshape.235), channel_id=1, replica_groups=mesh['space'=4,'freq'=8] {'freq'}, dimensions={0} | all-to-all | bytes 4718592 | tf_op jit(solution)/shard_map/all_to_all | solution.py:88
  517.1 4.9 copy.39
  (70 shorter events, 39.5 us)
Async XLA Ops:
  6.5 183.7 %all-gather.3.cloned.1.call-start = ((), (), s32[]{:S(2)}) async-start(), calls=%async_computation.4 | async-start | bytes 5308416 | tf_op jit(solution)/shard_map/all_gather | solution.py:65
  7.3 200.1 %all-gather.5.cloned.1.call-start = ((), (), s32[]{:S(2)}) async-start(), calls=%async_computation.5 | async-start | bytes 5308416 | tf_op jit(solution)/shard_map/all_gather | solution.py:66
  9.2 10.1 %collective-permute-start.1 = (f32[4,36,1,256]{3,1,2,0:T(8,128)S(1)}, f32[4,36,1,256]{3,1,2,0:T(8,128)S(1)}, u32[]{:S(2)}, u32[]{:S(2)}) collective-permute-start(f32[4,36,1,256]{3,1,2,0:T(8,128)S(1)} %copy.41), channel_id=1, source_target_pairs={{8,0},{16,8},{24,16},{9,1},{17,9},{25,17},{10,2},{18,10},{26,18},{... | collective-permute-start | bytes 442376 | tf_op jit(solution)/shard_map/ppermute | solution.py:24
  10.5 8.4 %copy-start.2 = (s32[32,256]{1,0:T(8,128)S(1)}, s32[32,256]{1,0:T(8,128)}, u32[]{:S(2)}) copy-start(s32[32,256]{1,0:T(8,128)} %param.9) | copy-start | bytes 98308
  10.5 8.4 %copy-start = (f32[32,256]{1,0:T(8,128)S(1)}, f32[32,256]{1,0:T(8,128)}, u32[]{:S(2)}) copy-start(f32[32,256]{1,0:T(8,128)} %param.13) | copy-start | bytes 98308
  10.5 8.4 %copy-start.1 = (f32[32,256]{1,0:T(8,128)S(1)}, f32[32,256]{1,0:T(8,128)}, u32[]{:S(2)}) copy-start(f32[32,256]{1,0:T(8,128)} %param.12) | copy-start | bytes 98308
  10.5 8.7 %collective-permute-start = (f32[4,36,1,256]{3,1,2,0:T(8,128)S(1)}, f32[4,36,1,256]{3,1,2,0:T(8,128)S(1)}, u32[]{:S(2)}, u32[]{:S(2)}) collective-permute-start(f32[4,36,1,256]{3,1,2,0:T(8,128)S(1)} %copy.40), channel_id=1, source_target_pairs={{0,8},{8,16},{16,24},{1,9},{9,17},{17,25},{2,10},{10,18},{18,26},{... | collective-permute-start | bytes 442376 | tf_op jit(solution)/shard_map/ppermute | solution.py:21
  13.8 5.4 %copy-start.4 = (f32[4]{0:T(128)S(1)}, f32[4]{0:T(128)}, u32[]{:S(2)}) copy-start(f32[4]{0:T(128)} %param.10) | copy-start | bytes 52
  19.3 5.4 %copy-start.3 = (f32[4]{0:T(128)S(1)}, f32[4]{0:T(128)}, u32[]{:S(2)}) copy-start(f32[4]{0:T(128)} %param.11) | copy-start | bytes 52
  33.6 4.9 slice-start.2
  35.1 3.4 slice-start.3
  296.1 2.2 slice-start.4
  296.1 2.5 slice-start.5
  299.8 2.6 collective-permute-start.2
  301.1 4.7 collective-permute-start.3
  320.1 4.8 slice-start
  321.6 3.4 slice-start.1
  513.5 2.2 slice-start.6
  513.5 2.5 slice-start.7
Sparse Core Ops, SparseCore 0:
  9.4 89.1 all-gather.2
  100.7 106.5 all-gather.4
where the time goes:
time: 538 us; the launch traced here: 529 us
  blocking collectives  347 us (64%)
  other arithmetic  54 us (10%)
  local copies, waits for them, and re-layouts  48.6 us (9%)
  matrix products  36.8 us (7%)
  waiting for transfers between devices  21.2 us (4%)
  between operations  14 us (3%)
  starting transfers between devices  7.1 us (1%)
    all_to_all x2, blocking collectives, body(): lax.all_to_all(scaled, 'freq', split_axis=2, concat_axis=0, tiled=True)  157 us
    all_to_all x2, blocking collectives, body(): lax.all_to_all(shaped, 'freq', split_axis=0, concat_axis=2, tiled=True)  114 us
    psum x2, blocking collectives, body(): point_total = lax.psum(partial_sum, 'freq')  75.9 us
    dot_general x2, matrix products, body(): lax.dot_general(out_whole, hidden, contract, preferred_element_type=jnp.f...  36.8 us
    mul x2, other arithmetic, transport(): turned = turned + jnp.roll(turn_neg * shifted, -1, axis=1)  18 us
    all_gather x1, waiting for transfers between devices, body(): lax.all_gather(w_out, 'freq', axis=0, tiled=True)  17.1 us
    unnamed x31, local copies, waits for them, and re-layouts  10.8 us
  transfers between devices with their start and end apart: 6, of which 2 were waited for; matrix products, arithmetic and copies ran while one was open for 7% of the time, Pallas kernels for 0%

commit v1 on v0

v1 whole, which is shorter than its diff:
```python
import math

import jax
import jax.numpy as jnp
from jax import lax
from jax.experimental import pallas as pl
from jax.experimental.pallas import tpu as pltpu
from jax.sharding import PartitionSpec as P

DIRS = 36
STEPS = 2
STEP_SCALE = 0.5
EPSILON = 1e-06
ROOT_MAX = 2.9
ENCODE = 32767.0 / ROOT_MAX
DECODE = ROOT_MAX / 32767.0
NCOEF = 7
BLOCK = 2 * DIRS
f32, bf16, i16 = jnp.float32, jnp.bfloat16, jnp.int16


def coefficients(courant, refract):
    angles = (jnp.arange(DIRS, dtype=f32) + 0.5) * (2.0 * math.pi / DIRS)
    cosine, sine = jnp.cos(angles), jnp.sin(angles)
    sx = courant[:, None] * cosine[None, :]
    sy = courant[:, None] * sine[None, :]
    keep = 1.0 - jnp.abs(sx) - jnp.abs(sy)
    parts = [
        keep,
        jnp.maximum(sx, 0.0),
        jnp.maximum(-sx, 0.0),
        jnp.maximum(sy, 0.0),
        jnp.maximum(-sy, 0.0),
        refract[:, None] * sine[None, :],
        refract[:, None] * cosine[None, :],
        jnp.zeros_like(sx),
    ]
    return jnp.stack(parts, axis=-1).reshape(-1, NCOEF + 1)


def encode(value):
    return (jnp.sqrt(value) * ENCODE + 0.5).astype(jnp.int32).astype(i16)


def decode(code):
    root = code.astype(jnp.int32).astype(f32) * DECODE
    return root * root


def spread(coef_ref, wide_ref, channels):
    @pl.loop(0, channels // BLOCK)
    def _(b):
        rows = pl.ds(pl.multiple_of(b * BLOCK, 8), BLOCK)
        part = coef_ref[rows, :]
        for k in range(NCOEF):
            wide_ref[k, rows, :] = jnp.broadcast_to(part[:, k : k + 1], (BLOCK, 128))


def transport(center, above, below, coefs, dx, dy, sea):
    rows, cols = center.shape
    lane = lax.broadcasted_iota(jnp.int32, (rows, cols), 1)
    west = jnp.where(lane == 0, 0.0, pltpu.roll(center, 1, 1))
    east = jnp.where(lane == cols - 1, 0.0, pltpu.roll(center, cols - 1, 1))
    keep, pos_x, neg_x, pos_y, neg_y, turn_x, turn_y = coefs
    shifted = center * keep + pos_x * above + neg_x * below + pos_y * west + neg_y * east
    turning = (turn_x * dx - turn_y * dy) * shifted
    forward = jnp.maximum(turning, 0.0)
    backward = forward - turning
    first = lax.broadcasted_iota(jnp.int32, (8, cols), 0)
    moved = pltpu.roll(forward, 1, 0)
    moved = jnp.concatenate(
        [
            jnp.where(first == 0, forward[DIRS - 1 : DIRS], moved[0:8]),
            moved[8:32],
            jnp.where(first == DIRS % 8, forward[2 * DIRS - 1 : 2 * DIRS], moved[32:40]),
            moved[40:72],
        ],
        axis=0,
    )
    other = pltpu.roll(backward, rows - 1, 0)
    other = jnp.concatenate(
        [
            other[0:32],
            jnp.where(first == (DIRS - 1) % 8, backward[0:1], other[32:40]),
            other[40:64],
            jnp.where(first == 7, backward[DIRS : DIRS + 1], other[64:72]),
        ],
        axis=0,
    )
    return (shifted - forward - backward + moved + other) * sea


def wide(ref, k, rows, cols):
    part = ref[k, rows, :]
    return jnp.concatenate([part] * (cols // 128), axis=1)


def first_kernel(groups, prows, spec_ref, low_ref, high_ref, coef_ref, dx_ref, dy_ref, sea_ref, out_ref, buf, coefw):
    channels, cols = low_ref.shape
    rows = groups * prows
    spread(coef_ref, coefw, channels)
    buf[0] = low_ref[...]
    buf[rows + 1] = high_ref[...]

    @pl.loop(0, rows)
    def _(r):
        for h in range(cols // 128):
            lanes = pl.ds(h * 128, 128)
            buf[r + 1, :, lanes] = spec_ref[h, pl.ds(r, channels, stride=rows), :]

    @pl.loop(0, groups)
    def _(g):
        @pl.loop(0, prows)
        def _(j):
            r = g * prows + j
            dx, dy, sea = (ref[pl.ds(r, 1), :] for ref in (dx_ref, dy_ref, sea_ref))
            for b in range(channels // BLOCK):
                part = pl.ds(b * BLOCK, BLOCK)
                coefs = [wide(coefw, k, part, cols) for k in range(NCOEF)]
                moved = transport(buf[r + 1, part, :], buf[r, part, :], buf[r + 2, part, :], coefs, dx, dy, sea)
                out_ref[g, j, part, :] = encode(moved)


def network(x_ref, hid_ref, win_ref, wout_ref, inverse, emit):
    hidden, channels = win_ref.shape
    mblock = min(512, hidden)
    for m in range(0, hidden, mblock):
        pre = jnp.dot(win_ref[m : m + mblock, :], x_ref[...], preferred_element_type=f32) * inverse
        act = 0.5 * pre * (1.0 + jnp.tanh(0.7978845608028654 * (pre + 0.044715 * pre * pre * pre)))
        hid_ref[m : m + mblock, :] = act.astype(bf16)
    cblock = 4 * BLOCK
    for c in range(0, channels, cblock):
        source = jnp.dot(wout_ref[c : c + cblock, :], hid_ref[...], preferred_element_type=f32)
        emit(c, cblock, jnp.exp(STEP_SCALE * jnp.tanh(source)))


def load_weights(groups, space, win_parts, wout_parts, win_ref, wout_ref, sem):
    copies = []
    spaces = len(win_parts)
    hidden = win_ref.shape[0]
    hpart = hidden // (groups * spaces)
    for n, part in enumerate(win_parts):
        for p in range(groups):
            row = pl.multiple_of(p * hpart * spaces + (space ^ n) * hpart, 8)
            slot = n * groups + p
            copies.append(
                pltpu.make_async_copy(part.at[pl.ds(p * hpart, hpart), :], win_ref.at[pl.ds(row, hpart), :], sem.at[slot])
            )
    many = spaces * groups
    for n, part in enumerate(wout_parts):
        size = part.shape[0]
        row = pl.multiple_of((space ^ n) * size, 8)
        copies.append(pltpu.make_async_copy(part, wout_ref.at[pl.ds(row, size), :], sem.at[many + n]))
    return copies


def step_one_kernel(groups, prows, many, space_ref, code_ref, *refs):
    win_parts, wout_parts = refs[:many], refs[many : 2 * many]
    field_ref, edge_ref, x_ref, hid_ref, win_ref, wout_ref, sem = refs[2 * many :]
    local = code_ref.shape[2]
    channels, cols = x_ref.shape
    copies = load_weights(groups, space_ref[0], win_parts, wout_parts, win_ref, wout_ref, sem)
    for copy in copies:
        copy.start()
    for copy in copies:
        copy.wait()

    @pl.loop(0, prows)
    def _(r):
        total = jnp.zeros((8, cols), f32)
        for q in range(groups):
            for b in range(local // BLOCK):
                part = pl.ds(b * BLOCK, BLOCK)
                at = pl.ds(q * local + b * BLOCK, BLOCK)
                value = decode(code_ref[q, r, part, :])
                field_ref[r, at, :] = value
                total = total + jnp.sum(value.reshape(BLOCK // 8, 8, cols), axis=0)
        total = jnp.sum(total, axis=0, keepdims=True)
        inverse = 1.0 / (total / channels + EPSILON)
        x_ref[...] = field_ref[r].astype(bf16)

        def emit(c, size, factor):
            part = pl.ds(c, size)
            field_ref[r, part, :] = field_ref[r, part, :] * factor

        network(x_ref, hid_ref, win_ref, wout_ref, inverse, emit)

        @pl.when(r == 0)
        def _():
            edge_ref[0] = encode(field_ref[r])

        @pl.when(r == prows - 1)
        def _():
            edge_ref[1] = encode(field_ref[r])


def step_two_kernel(groups, prows, many, space_ref, field_ref, low_ref, high_ref, coef_ref, dx_ref, dy_ref, sea_ref, *refs):
    win_parts, wout_parts = refs[:many], refs[many : 2 * many]
    out_ref, rows_ref, moved_ref, code_ref, coefw, x_ref, hid_ref, win_ref, wout_ref, sem = refs[2 * many :]
    local = out_ref.shape[2]
    channels, cols = x_ref.shape
    copies = load_weights(groups, space_ref[0], win_parts, wout_parts, win_ref, wout_ref, sem)
    for copy in copies:
        copy.start()
    spread(coef_ref, coefw, channels)
    rows_ref[0] = decode(low_ref[...])
    rows_ref[1] = decode(high_ref[...])
    for copy in copies:
        copy.wait()

    def one(r, above_ref, ra, below_ref, rb):
        dx, dy, sea = (ref[pl.ds(r, 1), :] for ref in (dx_ref, dy_ref, sea_ref))

        def blocks(b, total):
            part = pl.ds(pl.multiple_of(b * BLOCK, 8), BLOCK)
            coefs = [wide(coefw, k, part, cols) for k in range(NCOEF)]
            moved = transport(
                field_ref[r, part, :], above_ref[ra, part, :], below_ref[rb, part, :], coefs, dx, dy, sea
            )
            moved_ref[part, :] = moved
            return total + jnp.sum(moved.reshape(BLOCK // 8, 8, cols), axis=0)

        total = lax.fori_loop(0, channels // BLOCK, blocks, jnp.zeros((8, cols), f32))
        total = jnp.sum(total, axis=0, keepdims=True)
        inverse = 1.0 / (total / channels + EPSILON)
        x_ref[...] = moved_ref[...].astype(bf16)

        def emit(c, size, factor):
            part = pl.ds(c, size)
            moved_ref[part, :] = moved_ref[part, :] * factor

        network(x_ref, hid_ref, win_ref, wout_ref, inverse, emit)
        for q in range(groups):
            out_ref[q, r] = encode(moved_ref[pl.ds(q * local, local), :])

    if prows == 1:
        one(0, rows_ref, 0, rows_ref, 1)
        return
    one(0, rows_ref, 0, field_ref, 1)

    @pl.loop(1, prows - 1)
    def _(r):
        one(r, field_ref, r - 1, field_ref, r + 1)

    one(prows - 1, field_ref, prows - 2, rows_ref, 1)


def last_kernel(groups, prows, code_ref, out_ref):
    local, cols = code_ref.shape[2:]
    rows = groups * prows

    @pl.loop(0, groups)
    def _(g):
        @pl.loop(0, prows)
        def _(j):
            for b in range(local // BLOCK):
                value = decode(code_ref[g, j, pl.ds(b * BLOCK, BLOCK), :])
                start = (b * BLOCK) * rows + g * prows + j
                for h in range(cols // 128):
                    out_ref[h, pl.ds(start, BLOCK, stride=rows), :] = value[:, h * 128 : (h + 1) * 128]


def exchange(array, axis, bit):
    count = lax.axis_size(axis)
    return lax.ppermute(array, axis, [(i, i ^ bit) for i in range(count)])


def gather_freq(piece, dim, count):
    bit = count // 2
    bits = []
    while bit >= 1:
        bits.append(bit)
        bit //= 2
    have = piece
    for bit in bits:
        have = jnp.concatenate([have, exchange(have, "freq", bit)], axis=dim)
    return have, bits


def gather_space(have, count):
    parts = [have]
    bit = count // 2
    order = [0]
    while bit >= 1:
        parts = parts + [exchange(part, "space", bit) for part in parts]
        order = order + [o ^ bit for o in order]
        bit //= 2
    ranked = sorted(zip(order, range(len(parts))))
    return [parts[n] for _, n in ranked]


def split3(value):
    high = lax.reduce_precision(value, 8, 7)
    rest = value - high
    middle = lax.reduce_precision(rest, 8, 7)
    return [part.astype(bf16) for part in (high, middle, rest - middle)]


def body(spectrum, land_sea, courant, refract, depth_dx, depth_dy, w_in, w_out):
    groups, spaces = lax.axis_size("freq"), lax.axis_size("space")
    space, freq = lax.axis_index("space"), lax.axis_index("freq")
    freqs, dirs, rows, cols = spectrum.shape
    local = freqs * dirs
    channels = local * groups
    prows = rows // groups
    hidden_local = w_in.shape[1]
    hidden = hidden_local * groups
    sea = land_sea.astype(f32)

    last = spectrum[:, :, rows - 1, :].reshape(local, cols)
    first = spectrum[:, :, 0, :].reshape(local, cols)
    up = [(i, i + 1) for i in range(spaces - 1)]
    low = lax.ppermute(last, "space", up)
    high = lax.ppermute(first, "space", [(b, a) for a, b in up])

    hpart, cpart = hidden_local // spaces, channels // spaces
    win_piece = lax.dynamic_slice_in_dim(w_in, space * hpart, hpart, 1).T
    numbers = jnp.stack(split3(courant) + split3(refract))
    numbers = jnp.pad(numbers, ((0, 2), (0, channels - freqs)))
    win_piece = jnp.concatenate([numbers, win_piece], axis=0)
    wout_piece = lax.dynamic_slice_in_dim(w_out, space * cpart, cpart, 1).T
    win_have, bits = gather_freq(win_piece[None], 0, groups)
    wout_have, _ = gather_freq(wout_piece, 1, groups)
    order = [0]
    for bit in bits:
        order = order + [o ^ bit for o in order]
    numbers = win_have[:, 0:6, 0:freqs].astype(f32)
    numbers = numbers[:, 0:6:3] + numbers[:, 1:6:3] + numbers[:, 2:6:3]
    inverse_order = [order.index(n) for n in range(groups)]
    absolute = jnp.take(numbers, jnp.array(inverse_order, jnp.int32)[jnp.arange(groups) ^ freq], axis=0)
    coef_all = coefficients(absolute[:, 0].reshape(-1), absolute[:, 1].reshape(-1))
    win_have = win_have[:, 8:, :].reshape(groups * hpart, channels)
    win_parts = gather_space(win_have, spaces)
    wout_parts = gather_space(wout_have, spaces)
    many = len(win_parts)
    space_arr = space.reshape(1).astype(jnp.int32)

    any_spec = pl.BlockSpec(memory_space=pl.ANY)
    vmem = pl.BlockSpec(memory_space=pltpu.VMEM)
    smem = pl.BlockSpec(memory_space=pltpu.SMEM)
    code_shape = jax.ShapeDtypeStruct((groups, prows, local, cols), i16)
    net_scratch = [
        pltpu.VMEM((channels, cols), bf16),
        pltpu.VMEM((hidden, cols), bf16),
        pltpu.VMEM((hidden, channels), bf16),
        pltpu.VMEM((channels, hidden), bf16),
        pltpu.SemaphoreType.DMA((many * (groups + 1),)),
    ]
    params = pltpu.CompilerParams(vmem_limit_bytes=60 * 1024 * 1024)

    halves = cols // 128
    flat = spectrum.reshape(local * rows, halves, 128).transpose(1, 0, 2)
    sent = pl.pallas_call(
        lambda *refs: first_kernel(groups, prows, *refs),
        in_specs=[vmem] * 7,
        out_specs=vmem,
        out_shape=code_shape,
        scratch_shapes=[pltpu.VMEM((rows + 2, local, cols), f32), pltpu.VMEM((NCOEF, local, 128), f32)],
        compiler_params=params,
        name="first",
    )(flat, low, high, coefficients(courant, refract), depth_dx, depth_dy, sea)
    arrived = lax.all_to_all(sent, "freq", 0, 0, tiled=True)

    field, edges = pl.pallas_call(
        lambda *refs: step_one_kernel(groups, prows, many, *refs),
        in_specs=[smem, vmem] + [any_spec] * (2 * many),
        out_specs=(vmem, vmem),
        out_shape=(
            jax.ShapeDtypeStruct((prows, channels, cols), f32),
            jax.ShapeDtypeStruct((2, channels, cols), i16),
        ),
        scratch_shapes=net_scratch,
        compiler_params=params,
        name="step_one",
    )(space_arr, arrived, *win_parts, *wout_parts)

    chain = [(i, i + 1) for i in range(spaces * groups - 1)]
    low = lax.ppermute(edges[1], ("space", "freq"), chain)
    high = lax.ppermute(edges[0], ("space", "freq"), [(b, a) for a, b in chain])
    mine = [lax.dynamic_slice_in_dim(a, freq * prows, prows, 0) for a in (depth_dx, depth_dy, sea)]
    sent = pl.pallas_call(
        lambda *refs: step_two_kernel(groups, prows, many, *refs),
        in_specs=[smem] + [vmem] * 7 + [any_spec] * (2 * many),
        out_specs=vmem,
        out_shape=code_shape,
        scratch_shapes=[
            pltpu.VMEM((2, channels, cols), f32),
            pltpu.VMEM((channels, cols), f32),
            pltpu.VMEM((8, 128), i16),
            pltpu.VMEM((NCOEF, channels, 128), f32),
        ]
        + net_scratch,
        compiler_params=params,
        name="step_two",
    )(space_arr, field, low, high, coef_all, *mine, *win_parts, *wout_parts)
    arrived = lax.all_to_all(sent, "freq", 0, 0, tiled=True)

    out = pl.pallas_call(
        lambda *refs: last_kernel(groups, prows, *refs),
        in_specs=[vmem],
        out_specs=vmem,
        out_shape=jax.ShapeDtypeStruct((halves, local * rows, 128), f32),
        compiler_params=params,
        name="last",
    )(arrived)
    return out.transpose(1, 0, 2).reshape(freqs, dirs, rows, cols)


def solution(mesh):
    placed = (
        P("freq", None, "space", None),
        P("space", None),
        P("freq"),
        P("freq"),
        P("space", None),
        P("space", None),
        P(None, "freq"),
        P("freq", None),
    )
    return jax.shard_map(
        body, mesh=mesh, in_specs=placed, out_specs=P("freq", None, "space", None), check_vma=False
    )
```

time: 538 us -> 351 us (0.65); the launches traced: 529 us -> 350 us
  blocking collectives: 347 us -> 61.7 us
  waiting for transfers between devices: 21.2 us -> 127 us
  Pallas kernels: 0 us -> 80.7 us
  other arithmetic: 54 us -> 2.08 us
  matrix products: 36.8 us -> 0 us
  starting transfers between devices: 7.1 us -> 28.7 us
  between operations: 14 us -> 0.37 us
    all_to_all x4 -> x1, blocking collectives: 271 us -> 61.7 us  [body(): arrived = lax.all_to_all(sent, 'freq', 0, 0, tiled=True)]
    ppermute x4 -> x16, waiting for transfers between devices: 3.39 us -> 127 us  [the longest x12 105 us: exchange(): return lax.ppermute(array, axis, [(i, i ^ bit) for i in range(count)])]
    pallas_call x0 -> x4, Pallas kernels: none -> 80.7 us  [the longest x1 32.3 us: body(): pl.pallas_call(lambda *refs: step_two_kernel(groups, prows, many, *refs),...]
    psum x2 -> x0, blocking collectives: 75.9 us -> none  [body(): point_total = lax.psum(partial_sum, 'freq')]
    dot_general x2 -> x0, matrix products: 36.8 us -> none  [body(): lax.dot_general(out_whole, hidden, contract, preferred_element_type=jnp.f...]
    mul x6 -> x0, other arithmetic: 22.5 us -> none  [the longest x2 18 us: transport(): turned = turned + jnp.roll(turn_neg * shifted, -1, axis=1)]
    all_gather x2 -> x0, waiting for transfers between devices: 17.1 us -> none  [the longest x1 17.1 us: body(): lax.all_gather(w_out, 'freq', axis=0, tiled=True)]
    transpose x0 -> x1, local copies, waits for them, and re-layouts: none -> 15.6 us  [body(): return out.transpose(1, 0, 2).reshape(freqs, dirs, rows, cols)]
  transfers between devices with their start and end apart: 6 -> 17, of which waited for: 2 -> 7; matrix products, arithmetic and copies ran while one was open for 7% -> 6% of each run, Pallas kernels for 0% -> 5%
where the time goes in v1:
time: 351 us; the launch traced here: 350 us
  waiting for transfers between devices  127 us (36%)
  Pallas kernels  80.7 us (23%)
  blocking collectives  61.7 us (18%)
  local copies, waits for them, and re-layouts  49.2 us (14%)
  starting transfers between devices  28.7 us (8%)
    ppermute x12, waiting for transfers between devices, exchange(): return lax.ppermute(array, axis, [(i, i ^ bit) for i in range(count)])  105 us
    all_to_all x1, blocking collectives, body(): arrived = lax.all_to_all(sent, 'freq', 0, 0, tiled=True)  61.7 us
    pallas_call x1, Pallas kernels, body(): pl.pallas_call(lambda *refs: step_two_kernel(groups, prows, many, *refs),...  32.3 us
    ppermute x1, waiting for transfers between devices, body(): low = lax.ppermute(edges[1], ('space', 'freq'), chain)  22.5 us
    pallas_call x1, Pallas kernels, body(): pl.pallas_call(lambda *refs: step_one_kernel(groups, prows, many, *refs),...  21.4 us
    pallas_call x1, Pallas kernels, body(): pl.pallas_call(lambda *refs: first_kernel(groups, prows, *refs), in_specs...  18.1 us
    transpose x1, local copies, waits for them, and re-layouts, body(): return out.transpose(1, 0, 2).reshape(freqs, dirs, rows, cols)  15.6 us
    ppermute x12, starting transfers between devices, exchange(): return lax.ppermute(array, axis, [(i, i ^ bit) for i in range(count)])  14.3 us
  transfers between devices with their start and end apart: 17, of which 7 were waited for; matrix products, arithmetic and copies ran while one was open for 6% of the time, Pallas kernels for 5%

profile of v1, /device:TPU:0, one launch (start us, length us, event | category | flops | bytes accessed | tf_op | source)
XLA Modules:
  0.0 350.1 jit_solution(11405360284383108238)
XLA Ops:
  0.0 2.4 slice_reduce_fusion
  2.5 2.4 collective-permute-start
  6.7 3.5 collective-permute-start.2
  12.0 6.7 %reshape.524 = f32[4608,2,128]{2,1,0:T(2,128)} reshape(f32[4,36,32,256]{3,2,1,0:T(8,128)} %param.9) | data formatting | bytes 9437184 | tf_op jit(solution)/shard_map/reshape | solution.py:352
  18.8 4.8 %copy.45 = f32[4608,2,128]{2,0,1:T(8,128)} copy(f32[4608,2,128]{2,1,0:T(2,128)} %reshape.524) | data formatting | bytes 9437184 | tf_op jit(solution)/shard_map/reshape | solution.py:352
  25.7 18.1 %first.1 = s16[8,4,144,256]{3,2,1,0:T(8,128)(2,1)} custom-call(f32[2,4608,128]{2,1,0:T(8,128)} %bitcast.46, f32[144,256]{1,0:T(8,128)} %copy-done.8, f32[144,256]{1,0:T(8,128)} %copy-done.9, f32[144,8]{1,0:T(8,128)} %copy.35.refs_3_, f32[32,256]{1,0:T(8,128)} %refs_4_.1, f32[32,256]{1,0:T(8,128)} %refs_5_.1, f32[32,256]{1,0:T(8,128)} %convert_element_type.26.refs_6_), custom_call_target="tpu_custom_call" | custom-call | tf_op jit(solution)/shard_map/first/pallas_call | solution.py:353
  43.7 6.1 %all-to-all-start = ((s16[8,4,144,256]{3,2,1,0:T(8,128)(2,1)}), s16[8,4,144,256]{3,2,1,0:T(8,128)(2,1)}, u32[]{:S(2)}, u32[]{:S(2)}) async-start(s16[8,4,144,256]{3,2,1,0:T(8,128)(2,1)} %first.1), calls=%async_computation | async-start | bytes 4718592 | tf_op jit(solution)/shard_map/all_to_all | solution.py:362
  49.9 2.1 collective-permute-start.9
  52.1 44.0 %collective-permute-done.9 = bf16[288,512]{1,0:T(8,128)(2,1)S(1)} collective-permute-done((bf16[288,512]{1,0:T(8,128)(2,1)S(1)}, bf16[288,512]{1,0:T(8,128)(2,1)S(1)}, u32[]{:S(2)}, u32[]{:S(2)}) %collective-permute-start.9) | collective-permute-done | bytes 294944 | tf_op jit(solution)/shard_map/ppermute | solution.py:265
  96.2 1.8 collective-permute-start.10
  98.0 5.3 %collective-permute-done.3 = bf16[2,72,1152]{2,1,0:T(8,128)(2,1)S(1)} collective-permute-done((bf16[2,72,1152]{2,1,0:T(8,128)(2,1)S(1)}, bf16[2,72,1152]{2,1,0:T(8,128)(2,1)S(1)}, u32[]{:S(2)}, u32[]{:S(2)}) %collective-permute-start.3) | collective-permute-done | bytes 331808 | tf_op jit(solution)/shard_map/ppermute | solution.py:265
  105.1 6.5 %collective-permute-done.10 = bf16[288,1024]{1,0:T(8,128)(2,1)S(1)} collective-permute-done((bf16[288,1024]{1,0:T(8,128)(2,1)S(1)}, bf16[288,1024]{1,0:T(8,128)(2,1)S(1)}, u32[]{:S(2)}, u32[]{:S(2)}) %collective-permute-start.10) | collective-permute-done | bytes 589856 | tf_op jit(solution)/shard_map/ppermute | solution.py:265
  111.7 3.8 %collective-permute-start.12 = (bf16[288,2048]{1,0:T(8,128)(2,1)S(1)}, bf16[288,2048]{1,0:T(8,128)(2,1)}, u32[]{:S(2)}, u32[]{:S(2)}) collective-permute-start(bf16[288,2048]{1,0:T(8,128)(2,1)S(1)} %pad_maximum_fusion.1.refs_6_.refs_12_), channel_id=1, source_target_pairs={{0,16},{8,24},{16,0},{24,8},{1,17},{9,25},{17,1},{25,9},{2,18},{10... | collective-permute-start | bytes 3538952 | tf_op jit(solution)/shard_map/ppermute | solution.py:265
  115.5 10.3 %collective-permute-done.4 = bf16[4,72,1152]{2,1,0:T(8,128)(2,1)S(1)} collective-permute-done((bf16[4,72,1152]{2,1,0:T(8,128)(2,1)S(1)}, bf16[4,72,1152]{2,1,0:T(8,128)(2,1)S(1)}, u32[]{:S(2)}, u32[]{:S(2)}) %collective-permute-start.4) | collective-permute-done | bytes 663584 | tf_op jit(solution)/shard_map/ppermute | solution.py:265
  128.2 14.2 %collective-permute-done.12.refs_8_.refs_14_ = bf16[288,2048]{1,0:T(8,128)(2,1)} collective-permute-done((bf16[288,2048]{1,0:T(8,128)(2,1)S(1)}, bf16[288,2048]{1,0:T(8,128)(2,1)}, u32[]{:S(2)}, u32[]{:S(2)}) %collective-permute-start.12) | collective-permute-done | bytes 1179680 | tf_op jit(solution)/shard_map/ppermute | solution.py:265
  142.4 24.5 %collective-permute-done.6.refs_4_.refs_10_ = bf16[512,1152]{1,0:T(8,128)(2,1)} collective-permute-done((bf16[512,1152]{1,0:T(8,128)(2,1)S(1)}, bf16[512,1152]{1,0:T(8,128)(2,1)}, u32[]{:S(2)}, u32[]{:S(2)}) %collective-permute-start.6) | collective-permute-done | bytes 1179680 | tf_op jit(solution)/shard_map/ppermute | solution.py:265
  171.6 21.4 %step_one.1 = (f32[4,1152,256]{2,1,0:T(8,128)}, s16[2,1152,256]{2,1,0:T(8,128)(2,1)}) custom-call(s32[1]{0:T(128)} %bitcast.refs_0_, s16[8,4,144,256]{3,2,1,0:T(8,128)(2,1)} %all-to-all-done.refs_1_, bf16[512,1152]{1,0:T(8,128)(2,1)} %bitcast.50, bf16[512,1152]{1,0:T(8,128)(2,1)} %collective-permute-done.5.refs_3_.refs_9_, ...), custom_call_target="tpu_custom_call" | custom-call | tf_op jit(solution)/shard_map/step_one/pallas_call | solution.py:364
  194.4 3.1 collective-permute-start.14
  200.8 22.5 %collective-permute-done.14.refs_2_ = s16[1152,256]{1,0:T(8,128)(2,1)S(1)} collective-permute-done((s16[1152,256]{1,0:T(8,128)(2,1)S(1)}, s16[1152,256]{1,0:T(8,128)(2,1)S(1)}, u32[]{:S(2)}, u32[]{:S(2)}) %collective-permute-start.14) | collective-permute-done | bytes 589856 | tf_op jit(solution)/shard_map/ppermute | solution.py:378
  224.4 32.3 %step_two.1 = s16[8,4,144,256]{3,2,1,0:T(8,128)(2,1)} custom-call(s32[1]{0:T(128)} %bitcast.refs_0_, f32[4,1152,256]{2,1,0:T(8,128)} %get-tuple-element.7.refs_1_, s16[1152,256]{1,0:T(8,128)(2,1)} %copy-done.6, s16[1152,256]{1,0:T(8,128)(2,1)} %copy-done.7, f32[1152,8]{1,0:T(8,128)} %copy.38.refs_4_, f32[4,256]{1,0:T(4,128)} %constant_dynamic-slice_fusion.2.refs_5_, ...), custom_call_target="tpu_custom_call" | custom-call | tf_op jit(solution)/shard_map/step_two/pallas_call | solution.py:381
  256.6 61.7 %all_to_all.10.refs_0_ = s16[8,4,144,256]{3,2,1,0:T(8,128)(2,1)} all-to-all(s16[8,4,144,256]{3,2,1,0:T(8,128)(2,1)} %step_two.1), channel_id=1, replica_groups=mesh['space'=4,'freq'=8] {'freq'}, dimensions={0} | all-to-all | bytes 4718592 | tf_op jit(solution)/shard_map/all_to_all | solution.py:396
  318.4 8.9 %last.1 = f32[2,4608,128]{2,1,0:T(8,128)} custom-call(s16[8,4,144,256]{3,2,1,0:T(8,128)(2,1)} %all_to_all.10.refs_0_), custom_call_target="tpu_custom_call" | custom-call | tf_op jit(solution)/shard_map/last/pallas_call | solution.py:398
  327.3 15.6 %copy.39 = f32[4608,2,128]{2,1,0:T(2,128)} copy(f32[4608,2,128]{2,0,1:T(8,128)} %bitcast.47) | data formatting | bytes 9437184 | tf_op jit(solution)/shard_map/transpose | solution.py:406
  342.9 7.2 %reshape.526 = f32[4,36,32,256]{3,2,1,0:T(8,128)} reshape(f32[4608,2,128]{2,1,0:T(2,128)} %copy.39) | data formatting | bytes 9437184 | tf_op jit(solution)/shard_map/reshape | solution.py:406
  (108 shorter events, 20.5 us)
Async XLA Ops:
  0.0 6.2 %copy-start = (bf16[1152,256]{1,0:T(8,128)(2,1)S(1)}, bf16[1152,256]{1,0:T(8,128)(2,1)}, u32[]{:S(2)}) copy-start(bf16[1152,256]{1,0:T(8,128)(2,1)} %param.15) | copy-start | bytes 1769476
  0.0 6.6 %copy-start.11 = (f32[4]{0:T(128)S(1)}, f32[4]{0:T(128)}, u32[]{:S(2)}) copy-start(f32[4]{0:T(128)} %param.11) | copy-start | bytes 52
  0.0 6.6 %copy-start.12 = (f32[4]{0:T(128)S(1)}, f32[4]{0:T(128)}, u32[]{:S(2)}) copy-start(f32[4]{0:T(128)} %param.12) | copy-start | bytes 52
  2.5 22.5 %collective-permute-start = (f32[144,256]{1,0:T(8,128)S(1)}, f32[144,256]{1,0:T(8,128)S(1)}, u32[]{:S(2)}, u32[]{:S(2)}) collective-permute-start(f32[144,256]{1,0:T(8,128)S(1)} %reshape_squeeze.6), channel_id=1, source_target_pairs={{0,8},{8,16},{16,24},{1,9},{9,17},{17,25},{2,10},{10,18},{18,26},{... | collective-permute-start | bytes 442376 | tf_op jit(solution)/shard_map/ppermute | solution.py:313
  4.9 20.0 %collective-permute-start.1 = (f32[144,256]{1,0:T(8,128)S(1)}, f32[144,256]{1,0:T(8,128)S(1)}, u32[]{:S(2)}, u32[]{:S(2)}) collective-permute-start(f32[144,256]{1,0:T(8,128)S(1)} %reshape_squeeze.7), channel_id=1, source_target_pairs={{8,0},{16,8},{24,16},{9,1},{17,9},{25,17},{10,2},{18,10},{26,18},{... | collective-permute-start | bytes 442376 | tf_op jit(solution)/shard_map/ppermute | solution.py:314
  6.7 45.3 %collective-permute-start.2 = (bf16[1,72,1152]{2,1,0:T(8,128)(2,1)S(1)}, bf16[1,72,1152]{2,1,0:T(8,128)(2,1)S(1)}, u32[]{:S(2)}, u32[]{:S(2)}) collective-permute-start(bf16[1,72,1152]{2,1,0:T(8,128)(2,1)S(1)} %fusion.2), channel_id=1, source_target_pairs={{0,4},{1,5},{2,6},{3,7},{4,0},{5,1},{6,2},{7,3},{8,12},{9,13},{10,... | collective-permute-start | bytes 497672 | tf_op jit(solution)/shard_map/ppermute | solution.py:265
  11.3 38.5 %collective-permute-start.8 = (bf16[288,256]{1,0:T(8,128)(2,1)S(1)}, bf16[288,256]{1,0:T(8,128)(2,1)S(1)}, u32[]{:S(2)}, u32[]{:S(2)}) collective-permute-start(bf16[288,256]{1,0:T(8,128)(2,1)S(1)} %bitcast.52), channel_id=1, source_target_pairs={{0,4},{1,5},{2,6},{3,7},{4,0},{5,1},{6,2},{7,3},{8,12},{9,13},{10,... | collective-permute-start | bytes 442376 | tf_op jit(solution)/shard_map/ppermute | solution.py:265
  43.7 127.9 %all-to-all-start = ((s16[8,4,144,256]{3,2,1,0:T(8,128)(2,1)}), s16[8,4,144,256]{3,2,1,0:T(8,128)(2,1)}, u32[]{:S(2)}, u32[]{:S(2)}) async-start(s16[8,4,144,256]{3,2,1,0:T(8,128)(2,1)} %first.1), calls=%async_computation | async-start | bytes 4718592 | tf_op jit(solution)/shard_map/all_to_all | solution.py:362
  49.9 46.2 %collective-permute-start.9 = (bf16[288,512]{1,0:T(8,128)(2,1)S(1)}, bf16[288,512]{1,0:T(8,128)(2,1)S(1)}, u32[]{:S(2)}, u32[]{:S(2)}) collective-permute-start(bf16[288,512]{1,0:T(8,128)(2,1)S(1)} %pad_maximum_fusion.5), channel_id=1, source_target_pairs={{0,2},{1,3},{2,0},{3,1},{4,6},{5,7},{6,4},{7,5},{8,10},{9,11},{10,... | collective-permute-start | bytes 884744 | tf_op jit(solution)/shard_map/ppermute | solution.py:265
  52.0 73.8 %copy-start.5 = (bf16[1,72,1152]{2,1,0:T(8,128)(2,1)}, bf16[1,72,1152]{2,1,0:T(8,128)(2,1)S(1)}, u32[]{:S(2)}) copy-start(bf16[1,72,1152]{2,1,0:T(8,128)(2,1)S(1)} %collective-permute-done.2) | copy-start | bytes 497668
  52.0 51.2 %collective-permute-start.3 = (bf16[2,72,1152]{2,1,0:T(8,128)(2,1)S(1)}, bf16[2,72,1152]{2,1,0:T(8,128)(2,1)S(1)}, u32[]{:S(2)}, u32[]{:S(2)}) collective-permute-start(bf16[2,72,1152]{2,1,0:T(8,128)(2,1)S(1)} %pad_maximum_fusion.4), channel_id=1, source_target_pairs={{0,2},{1,3},{2,0},{3,1},{4,6},{5,7},{6,4},{7,5},{8,10},{9,11},{10,... | collective-permute-start | bytes 995336 | tf_op jit(solution)/shard_map/ppermute | solution.py:265
  96.2 15.4 %collective-permute-start.10 = (bf16[288,1024]{1,0:T(8,128)(2,1)S(1)}, bf16[288,1024]{1,0:T(8,128)(2,1)S(1)}, u32[]{:S(2)}, u32[]{:S(2)}) collective-permute-start(bf16[288,1024]{1,0:T(8,128)(2,1)S(1)} %pad_maximum_fusion.3), channel_id=1, source_target_pairs={{0,1},{1,0},{2,3},{3,2},{4,5},{5,4},{6,7},{7,6},{8,9},{9,8},{10,11... | collective-permute-start | bytes 1769480 | tf_op jit(solution)/shard_map/ppermute | solution.py:265
  103.3 22.5 %collective-permute-start.4 = (bf16[4,72,1152]{2,1,0:T(8,128)(2,1)S(1)}, bf16[4,72,1152]{2,1,0:T(8,128)(2,1)S(1)}, u32[]{:S(2)}, u32[]{:S(2)}) collective-permute-start(bf16[4,72,1152]{2,1,0:T(8,128)(2,1)S(1)} %pad_maximum_fusion.2), channel_id=1, source_target_pairs={{0,1},{1,0},{2,3},{3,2},{4,5},{5,4},{6,7},{7,6},{8,9},{9,8},{10,11... | collective-permute-start | bytes 1990664 | tf_op jit(solution)/shard_map/ppermute | solution.py:265
  111.7 15.2 %copy-start.2 = (bf16[288,2048]{1,0:T(8,128)(2,1)}, bf16[288,2048]{1,0:T(8,128)(2,1)S(1)}, u32[]{:S(2)}) copy-start(bf16[288,2048]{1,0:T(8,128)(2,1)S(1)} %pad_maximum_fusion.1.refs_6_.refs_12_) | copy-start | bytes 3538948
  111.7 30.7 %collective-permute-start.12 = (bf16[288,2048]{1,0:T(8,128)(2,1)S(1)}, bf16[288,2048]{1,0:T(8,128)(2,1)}, u32[]{:S(2)}, u32[]{:S(2)}) collective-permute-start(bf16[288,2048]{1,0:T(8,128)(2,1)S(1)} %pad_maximum_fusion.1.refs_6_.refs_12_), channel_id=1, source_target_pairs={{0,16},{8,24},{16,0},{24,8},{1,17},{9,25},{17,1},{25,9},{2,18},{10... | collective-permute-start | bytes 3538952 | tf_op jit(solution)/shard_map/ppermute | solution.py:265
  126.0 40.9 %copy-start.1 = (s32[8]{0:T(128)S(1)}, s32[8]{0:T(128)}, u32[]{:S(2)}) copy-start(s32[8]{0:T(128)} %constant.55.clone) | copy-start | bytes 100
  126.7 45.0 %copy-start.3 = (bf16[8,64,1152]{2,1,0:T(8,128)(2,1)}, bf16[8,64,1152]{2,1,0:T(8,128)(2,1)S(1)}, u32[]{:S(2)}) copy-start(bf16[8,64,1152]{2,1,0:T(8,128)(2,1)S(1)} %slice.48) | copy-start | bytes 3538948
  126.7 40.2 %collective-permute-start.6 = (bf16[512,1152]{1,0:T(8,128)(2,1)S(1)}, bf16[512,1152]{1,0:T(8,128)(2,1)}, u32[]{:S(2)}, u32[]{:S(2)}) collective-permute-start(bf16[512,1152]{1,0:T(8,128)(2,1)S(1)} %bitcast.48), channel_id=1, source_target_pairs={{0,16},{8,24},{16,0},{24,8},{1,17},{9,25},{17,1},{25,9},{2,18},{10... | collective-permute-start | bytes 3538952 | tf_op jit(solution)/shard_map/ppermute | solution.py:265
  126.9 44.6 %collective-permute-start.11 = (bf16[288,2048]{1,0:T(8,128)(2,1)S(1)}, bf16[288,2048]{1,0:T(8,128)(2,1)}, u32[]{:S(2)}, u32[]{:S(2)}) collective-permute-start(bf16[288,2048]{1,0:T(8,128)(2,1)S(1)} %pad_maximum_fusion.1.refs_6_.refs_12_), channel_id=1, source_target_pairs={{0,8},{8,0},{16,24},{24,16},{1,9},{9,1},{17,25},{25,17},{2,10},{10... | collective-permute-start | bytes 3538952 | tf_op jit(solution)/shard_map/ppermute | solution.py:265
  128.1 43.5 %collective-permute-start.5 = (bf16[512,1152]{1,0:T(8,128)(2,1)S(1)}, bf16[512,1152]{1,0:T(8,128)(2,1)}, u32[]{:S(2)}, u32[]{:S(2)}) collective-permute-start(bf16[512,1152]{1,0:T(8,128)(2,1)S(1)} %bitcast.49), channel_id=1, source_target_pairs={{0,8},{8,0},{16,24},{24,16},{1,9},{9,1},{17,25},{25,17},{2,10},{10... | collective-permute-start | bytes 3538952 | tf_op jit(solution)/shard_map/ppermute | solution.py:265
  142.4 29.2 %collective-permute-start.13 = (bf16[288,2048]{1,0:T(8,128)(2,1)}, bf16[288,2048]{1,0:T(8,128)(2,1)}, u32[]{:S(2)}, u32[]{:S(2)}) collective-permute-start(bf16[288,2048]{1,0:T(8,128)(2,1)} %collective-permute-done.12.refs_8_.refs_14_), channel_id=1, source_target_pairs={{0,8},{8,0},{16,24},{24,16},{1,9},{9,1},{17,25},{25,17},{2,10},{10... | collective-permute-start | bytes 3538952 | tf_op jit(solution)/shard_map/ppermute | solution.py:265
  166.9 4.7 %collective-permute-start.7 = (bf16[512,1152]{1,0:T(8,128)(2,1)}, bf16[512,1152]{1,0:T(8,128)(2,1)}, u32[]{:S(2)}, u32[]{:S(2)}) collective-permute-start(bf16[512,1152]{1,0:T(8,128)(2,1)} %collective-permute-done.6.refs_4_.refs_10_), channel_id=1, source_target_pairs={{0,8},{8,0},{16,24},{24,16},{1,9},{9,1},{17,25},{25,17},{2,10},{10... | collective-permute-start | bytes 3538952 | tf_op jit(solution)/shard_map/ppermute | solution.py:265
  194.4 28.9 %collective-permute-start.14 = (s16[1152,256]{1,0:T(8,128)(2,1)S(1)}, s16[1152,256]{1,0:T(8,128)(2,1)S(1)}, u32[]{:S(2)}, u32[]{:S(2)}) collective-permute-start(s16[1152,256]{1,0:T(8,128)(2,1)S(1)} %get-tuple-element.14), channel_id=1, source_target_pairs={{0,1},{1,2},{2,3},{3,4},{4,5},{5,6},{6,7},{7,8},{8,9},{9,10},{10,1... | collective-permute-start | bytes 1769480 | tf_op jit(solution)/shard_map/ppermute | solution.py:378
  197.5 25.8 %collective-permute-start.15 = (s16[1152,256]{1,0:T(8,128)(2,1)S(1)}, s16[1152,256]{1,0:T(8,128)(2,1)S(1)}, u32[]{:S(2)}, u32[]{:S(2)}) collective-permute-start(s16[1152,256]{1,0:T(8,128)(2,1)S(1)} %get-tuple-element.13), channel_id=1, source_target_pairs={{1,0},{2,1},{3,2},{4,3},{5,4},{6,5},{7,6},{8,7},{9,8},{10,9},{11,1... | collective-permute-start | bytes 1769480 | tf_op jit(solution)/shard_map/ppermute | solution.py:379
  (6 other events, 9.7 us)
